TPU v7x, 32 devices: a whole 2x2x4 slice. The times are simulated.
32 devices in a mesh: rep: 2 (over y), shard: 16 (over z, x, core).
Axes of the slice: x: 2, y: 2, z: 4, core: 2. Of those that a mesh axis runs over, the one named last changes fastest.
Arguments:
- images: bfloat16 [32, 14, 14, 512], P(('rep', 'shard')), may hold values from -6 to 6
- cotangent: bfloat16 [32, 14, 14, 512], P(('rep', 'shard')), may hold values from -6 to 6
- regions: int32 [32, 14, 14], P(('rep', 'shard')), may hold values from 0 to 8, as said below
- w_qkv: bfloat16 [2, 512, 1536], P(None, 'shard'), may hold values from -0.25 to 0.25
- w_proj: bfloat16 [2, 512, 512], P(None, 'shard'), may hold values from -0.75 to 0.75
- w_fc1: bfloat16 [2, 512, 2048], P(None, 'shard'), may hold values from -0.25 to 0.25
- w_fc2: bfloat16 [2, 2048, 512], P(None, 'shard'), may hold values from -0.125 to 0.125
- norm_gains: bfloat16 [2, 2, 512], P(None, None, 'shard'), may hold values from 0.5 to 1.5
- norm_shifts: bfloat16 [2, 2, 512], P(None, None, 'shard'), may hold values from -1.1953125 to 1.1953125
- branch_biases: bfloat16 [2, 4, 512], P(None, None, 'shard'), may hold values from -1.1953125 to 1.1953125
- fc1_bias: bfloat16 [2, 2048], P(None, 'shard'), may hold values from -1.1953125 to 1.1953125
- rel_table: bfloat16 [2, 169, 16], replicated, may hold values from -6 to 6
Outputs:
- images_out: bfloat16 [32, 14, 14, 512], P(('rep', 'shard'))
- images_grad: float32 [32, 14, 14, 512], P(('rep', 'shard'))
- grad_w_qkv: float32 [2, 512, 1536], P(None, 'shard')
- grad_w_proj: float32 [2, 512, 512], P(None, 'shard')
- grad_w_fc1: float32 [2, 512, 2048], P(None, 'shard')
- grad_w_fc2: float32 [2, 2048, 512], P(None, 'shard')
- grad_norm_gains: float32 [2, 2, 512], P(None, None, 'shard')
- grad_norm_shifts: float32 [2, 2, 512], P(None, None, 'shard')
- grad_branch_biases: float32 [2, 4, 512], P(None, None, 'shard')
- grad_fc1_bias: float32 [2, 2048], P(None, 'shard')
- grad_rel_table: float32 [2, 169, 16], replicated
Inputs may be any that keep to these rules, and one draw needn't show every extreme that they name: `regions`: in each image the ids are 3 * (row band) + (column band), the rows and the columns each cut into three bands of consecutive positions.
All inputs are finite; a program needn't handle non-finite values.
Results may differ from a plain program's by a relative error of at most 0.023.
Values may be sent and summed in bfloat16 or wider, within the bound.
A program may use at most 128 MiB of HBM per device.

v0:
```python
import jax
import jax.numpy as jnp
from jax import lax
from jax.sharding import PartitionSpec as P

SIDE = 14
WIN = 7
SHIFT = 3
eps = 1e-05
highest = lax.Precision.HIGHEST
inv_root_two = 0.7071067811865476
inv_root_two_pi = 0.3989422804014327


def layer_norm(values, norm_gain, norm_shift):
    row_mean = jnp.mean(values, axis=-1, keepdims=True)
    centred = values - row_mean
    row_var = jnp.mean(centred * centred, axis=-1, keepdims=True)
    return centred * lax.rsqrt(row_var + eps) * norm_gain + norm_shift


def times_transposed(left, right):
    return lax.dot_general(
        left, right, (((1,), (1,)), ((), ())), preferred_element_type=jnp.float32
    )


def transposed_times(left, right):
    return lax.dot_general(
        left, right, (((0,), (0,)), ((), ())), preferred_element_type=jnp.float32
    )


def gelu_slope(pre_act):
    return 0.5 * (1.0 + lax.erf(pre_act * inv_root_two)) + pre_act * inv_root_two_pi * jnp.exp(
        -0.5 * pre_act * pre_act
    )


def to_windows(grid_data):
    image_count = grid_data.shape[0]
    per_side = SIDE // WIN
    trailing = grid_data.shape[3:]
    blocks = grid_data.reshape((image_count, per_side, WIN, per_side, WIN) + trailing)
    blocks = jnp.swapaxes(blocks, 2, 3)
    return blocks.reshape((image_count * per_side * per_side, WIN * WIN) + trailing)


def from_windows(blocks, image_count):
    per_side = SIDE // WIN
    trailing = blocks.shape[2:]
    grid_data = blocks.reshape((image_count, per_side, per_side, WIN, WIN) + trailing)
    grid_data = jnp.swapaxes(grid_data, 2, 3)
    return grid_data.reshape((image_count, SIDE, SIDE) + trailing)


def onehot_table():
    cell_ids = jnp.arange(WIN * WIN)
    cell_row = cell_ids // WIN
    cell_col = cell_ids % WIN
    table_side = 2 * WIN - 1
    rel_index = (cell_row[:, None] - cell_row[None, :] + WIN - 1) * table_side + (
        cell_col[:, None] - cell_col[None, :] + WIN - 1
    )
    rel_index = rel_index.reshape(-1)
    return (rel_index[:, None] == jnp.arange(table_side * table_side)[None, :]).astype(jnp.float32)


def replica_total(stacked):
    return (
        lax.psum(stacked[0].astype(jnp.bfloat16), "rep").astype(jnp.float32),
        lax.psum(stacked[1].astype(jnp.bfloat16), "rep").astype(jnp.float32),
        lax.psum(stacked[2].astype(jnp.bfloat16), "rep").astype(jnp.float32),
        lax.psum(stacked[3].astype(jnp.bfloat16), "rep").astype(jnp.float32),
        lax.psum(stacked[4].astype(jnp.bfloat16), "rep").astype(jnp.float32),
        lax.psum(stacked[5].astype(jnp.bfloat16), "rep").astype(jnp.float32),
        lax.psum(stacked[6].astype(jnp.bfloat16), "rep").astype(jnp.float32),
        lax.psum(stacked[7].astype(jnp.bfloat16), "rep").astype(jnp.float32),
    )


def body(
    images,
    cotangent,
    regions,
    w_qkv,
    w_proj,
    w_fc1,
    w_fc2,
    norm_gains,
    norm_shifts,
    branch_biases,
    fc1_bias,
    rel_table,
):
    layer_count = w_qkv.shape[0]
    image_count = images.shape[0]
    model_width = w_proj.shape[2]
    head_count = rel_table.shape[2]
    head_dim = model_width // head_count
    query_scale = head_dim ** (-0.5)
    column_scale = jnp.concatenate(
        [
            jnp.full((model_width,), query_scale, jnp.float32),
            jnp.ones((2 * model_width,), jnp.float32),
        ]
    )
    onehot = onehot_table()
    region_win = to_windows(regions)
    region_mask = jnp.where(region_win[:, :, None] == region_win[:, None, :], 0.0, -100.0).astype(
        jnp.float32
    )
    window_count = region_win.shape[0]
    tokens = window_count * WIN * WIN

    def score_bias(layer_num):
        table_rows = jnp.dot(onehot, rel_table[layer_num].astype(jnp.float32), precision=highest)
        bias_full = table_rows.T.reshape(head_count, WIN * WIN, WIN * WIN)[None]
        if layer_num % 2 == 1:
            bias_full = bias_full + region_mask[:, None]
        return bias_full

    def heads_of(flat):
        return flat.reshape(window_count, WIN * WIN, head_count, head_dim)

    residual = images.astype(jnp.float32)
    saved_acts = []
    kept_weights = []
    for layer_num in range(layer_count):
        shifted = layer_num % 2 == 1
        attn_w = (
            lax.all_gather(w_qkv[layer_num], "shard", axis=0, tiled=True),
            lax.all_gather(w_proj[layer_num], "shard", axis=0, tiled=True),
            lax.all_gather(norm_gains[layer_num], "shard", axis=1, tiled=True),
            lax.all_gather(norm_shifts[layer_num], "shard", axis=1, tiled=True),
            lax.all_gather(branch_biases[layer_num], "shard", axis=1, tiled=True),
        )
        mlp_w = (
            lax.all_gather(w_fc1[layer_num], "shard", axis=0, tiled=True),
            lax.all_gather(w_fc2[layer_num], "shard", axis=0, tiled=True),
            lax.all_gather(fc1_bias[layer_num], "shard", axis=0, tiled=True),
        )
        kept_weights.append((attn_w, mlp_w))
        wqkv, wproj, gains, shifts, biases = attn_w
        gains = gains.astype(jnp.float32)
        shifts = shifts.astype(jnp.float32)
        biases = biases.astype(jnp.float32)
        normed = layer_norm(residual, gains[0], shifts[0]).astype(jnp.bfloat16)
        if shifted:
            normed = jnp.roll(normed, (-SHIFT, -SHIFT), axis=(1, 2))
        window_rows = to_windows(normed).reshape(tokens, model_width)
        projected = jnp.dot(window_rows, wqkv, preferred_element_type=jnp.float32)
        queries = heads_of(
            ((projected[:, :model_width] + biases[0]) * query_scale).astype(jnp.bfloat16)
        )
        key_rows = heads_of(projected[:, model_width : 2 * model_width].astype(jnp.bfloat16))
        values = heads_of((projected[:, 2 * model_width :] + biases[1]).astype(jnp.bfloat16))
        scores = jnp.einsum(
            "nqhd,nkhd->nhqk", queries, key_rows, preferred_element_type=jnp.float32
        ) + score_bias(layer_num)
        row_max = jnp.max(scores, axis=-1, keepdims=True)
        log_total = row_max + jnp.log(jnp.sum(jnp.exp(scores - row_max), axis=-1, keepdims=True))
        attn_probs = jnp.exp(scores - log_total).astype(jnp.bfloat16)
        mixed_rows = jnp.einsum(
            "nhqk,nkhd->nqhd", attn_probs, values, preferred_element_type=jnp.float32
        )
        mixed_rows = mixed_rows.reshape(tokens, model_width).astype(jnp.bfloat16)
        branch = jnp.dot(mixed_rows, wproj, preferred_element_type=jnp.float32) + biases[2]
        branch = from_windows(branch.reshape(window_count, WIN * WIN, model_width), image_count)
        if shifted:
            branch = jnp.roll(branch, (SHIFT, SHIFT), axis=(1, 2))
        middle = residual + branch
        wfirst, wsecond, bias_first = mlp_w
        normed_mlp = (
            layer_norm(middle, gains[1], shifts[1]).astype(jnp.bfloat16).reshape(-1, model_width)
        )
        pre_act = jnp.dot(
            normed_mlp, wfirst, preferred_element_type=jnp.float32
        ) + bias_first.astype(jnp.float32)
        activated = jax.nn.gelu(pre_act, approximate=False).astype(jnp.bfloat16)
        mlp_out = jnp.dot(activated, wsecond, preferred_element_type=jnp.float32) + biases[3]
        saved_acts.append(
            (
                residual,
                window_rows,
                queries,
                key_rows,
                values,
                log_total,
                mixed_rows,
                middle,
                normed_mlp,
                pre_act,
                activated,
            )
        )
        residual = middle + mlp_out.reshape(middle.shape)
    images_out = residual.astype(jnp.bfloat16)
    upstream = cotangent.astype(jnp.float32)
    layer_grads = [None] * layer_count
    table_list = [None] * layer_count
    for layer_num in reversed(range(layer_count)):
        shifted = layer_num % 2 == 1
        (
            residual_in,
            window_rows,
            queries,
            key_rows,
            values,
            log_total,
            mixed_rows,
            middle,
            normed_mlp,
            pre_act,
            activated,
        ) = saved_acts[layer_num]
        wqkv, wproj, gains, shifts, biases = (
            lax.all_gather(w_qkv[layer_num], "shard", axis=0, tiled=True),
            lax.all_gather(w_proj[layer_num], "shard", axis=0, tiled=True),
            lax.all_gather(norm_gains[layer_num], "shard", axis=1, tiled=True),
            lax.all_gather(norm_shifts[layer_num], "shard", axis=1, tiled=True),
            lax.all_gather(branch_biases[layer_num], "shard", axis=1, tiled=True),
        )
        wfirst, wsecond, bias_first = (
            lax.all_gather(w_fc1[layer_num], "shard", axis=0, tiled=True),
            lax.all_gather(w_fc2[layer_num], "shard", axis=0, tiled=True),
            lax.all_gather(fc1_bias[layer_num], "shard", axis=0, tiled=True),
        )
        gains = gains.astype(jnp.float32)
        shifts = shifts.astype(jnp.float32)
        out_grad = upstream.astype(jnp.bfloat16).reshape(-1, model_width)
        grad_b_second = jnp.sum(out_grad.astype(jnp.float32), axis=0)
        grad_w_second = transposed_times(activated, out_grad)
        act_grad = times_transposed(out_grad, wsecond)
        pre_grad = (act_grad * gelu_slope(pre_act)).astype(jnp.bfloat16)
        grad_b_first = jnp.sum(pre_grad.astype(jnp.float32), axis=0)
        grad_w_first = transposed_times(normed_mlp, pre_grad)
        norm_grad = times_transposed(pre_grad, wfirst).reshape(middle.shape)
        norm_pull = jax.vjp(layer_norm, middle, gains[1], shifts[1])[1]
        middle_part, grad_gain_mlp, grad_shift_mlp = norm_pull(norm_grad)
        middle_grad = upstream + middle_part
        branch_grad = middle_grad
        if shifted:
            branch_grad = jnp.roll(branch_grad, (-SHIFT, -SHIFT), axis=(1, 2))
        branch_rows = to_windows(branch_grad.astype(jnp.bfloat16)).reshape(tokens, model_width)
        grad_b_proj = jnp.sum(branch_rows.astype(jnp.float32), axis=0)
        grad_w_proj = transposed_times(mixed_rows, branch_rows)
        mixed_grad = heads_of(times_transposed(branch_rows, wproj).astype(jnp.bfloat16))
        scores = jnp.einsum(
            "nqhd,nkhd->nhqk", queries, key_rows, preferred_element_type=jnp.float32
        ) + score_bias(layer_num)
        attn_probs = jnp.exp(scores - log_total)
        prob_grad = jnp.einsum(
            "nqhd,nkhd->nhqk", mixed_grad, values, preferred_element_type=jnp.float32
        )
        value_grad = jnp.einsum(
            "nhqk,nqhd->nkhd",
            attn_probs.astype(jnp.bfloat16),
            mixed_grad,
            preferred_element_type=jnp.float32,
        ).astype(jnp.bfloat16)
        score_grad = (
            attn_probs * (prob_grad - jnp.sum(attn_probs * prob_grad, axis=-1, keepdims=True))
        ).astype(jnp.bfloat16)
        table_term = jnp.sum(score_grad.astype(jnp.float32), axis=0).reshape(head_count, -1).T
        table_list[layer_num] = jnp.dot(onehot.T, table_term, precision=highest)
        query_grad = jnp.einsum(
            "nhqk,nkhd->nqhd", score_grad, key_rows, preferred_element_type=jnp.float32
        ).astype(jnp.bfloat16)
        key_grad = jnp.einsum(
            "nhqk,nqhd->nkhd", score_grad, queries, preferred_element_type=jnp.float32
        ).astype(jnp.bfloat16)
        qkv_grad = jnp.concatenate(
            [
                query_grad.reshape(tokens, model_width),
                key_grad.reshape(tokens, model_width),
                value_grad.reshape(tokens, model_width),
            ],
            axis=1,
        )
        grad_w_proj_qkv = transposed_times(window_rows, qkv_grad) * column_scale[None, :]
        grad_b_query = (
            jnp.sum(query_grad.reshape(tokens, model_width).astype(jnp.float32), axis=0)
            * query_scale
        )
        grad_b_value = jnp.sum(value_grad.reshape(tokens, model_width).astype(jnp.float32), axis=0)
        rows_grad = times_transposed(qkv_grad[:, :model_width], wqkv[:, :model_width]) * query_scale
        rows_grad = rows_grad + times_transposed(qkv_grad[:, model_width:], wqkv[:, model_width:])
        normed_grad = from_windows(
            rows_grad.reshape(window_count, WIN * WIN, model_width), image_count
        )
        if shifted:
            normed_grad = jnp.roll(normed_grad, (SHIFT, SHIFT), axis=(1, 2))
        first_pull = jax.vjp(layer_norm, residual_in, gains[0], shifts[0])[1]
        input_part, grad_gain_attn, grad_shift_attn = first_pull(normed_grad)
        upstream = middle_grad + input_part
        gain_grads = jnp.stack([grad_gain_attn, grad_gain_mlp])
        shift_grads = jnp.stack([grad_shift_attn, grad_shift_mlp])
        bias_grads = jnp.stack([grad_b_query, grad_b_value, grad_b_proj, grad_b_second])
        qkv_share, proj_share, gain_share, shift_share, bias_share = (
            lax.psum_scatter(
                grad_w_proj_qkv.astype(jnp.bfloat16), "shard", scatter_dimension=0, tiled=True
            ).astype(jnp.float32),
            lax.psum_scatter(
                grad_w_proj.astype(jnp.bfloat16), "shard", scatter_dimension=0, tiled=True
            ).astype(jnp.float32),
            lax.psum_scatter(
                gain_grads.astype(jnp.bfloat16), "shard", scatter_dimension=1, tiled=True
            ).astype(jnp.float32),
            lax.psum_scatter(
                shift_grads.astype(jnp.bfloat16), "shard", scatter_dimension=1, tiled=True
            ).astype(jnp.float32),
            lax.psum_scatter(
                bias_grads.astype(jnp.bfloat16), "shard", scatter_dimension=1, tiled=True
            ).astype(jnp.float32),
        )
        first_share, second_share, bfirst_share = (
            lax.psum_scatter(
                grad_w_first.astype(jnp.bfloat16), "shard", scatter_dimension=0, tiled=True
            ).astype(jnp.float32),
            lax.psum_scatter(
                grad_w_second.astype(jnp.bfloat16), "shard", scatter_dimension=0, tiled=True
            ).astype(jnp.float32),
            lax.psum_scatter(
                grad_b_first.astype(jnp.bfloat16), "shard", scatter_dimension=0, tiled=True
            ).astype(jnp.float32),
        )
        layer_grads[layer_num] = (
            qkv_share,
            proj_share,
            first_share,
            second_share,
            gain_share,
            shift_share,
            bias_share,
            bfirst_share,
        )
    stacked = [jnp.stack([layer_grads[n][m] for n in range(layer_count)]) for m in range(8)]
    summed = replica_total(stacked)
    table_total = lax.psum(jnp.stack(table_list), ("rep", "shard"))
    return (
        images_out,
        upstream,
        summed[0],
        summed[1],
        summed[2],
        summed[3],
        summed[4],
        summed[5],
        summed[6],
        summed[7],
        table_total,
    )


def solution(mesh):
    return jax.shard_map(
        body,
        mesh=mesh,
        in_specs=(
            P(("rep", "shard"), None, None, None),
            P(("rep", "shard"), None, None, None),
            P(("rep", "shard"), None, None),
            P(None, "shard", None),
            P(None, "shard", None),
            P(None, "shard", None),
            P(None, "shard", None),
            P(None, None, "shard"),
            P(None, None, "shard"),
            P(None, None, "shard"),
            P(None, "shard"),
            P(),
        ),
        out_specs=(
            P(("rep", "shard"), None, None, None),
            P(("rep", "shard"), None, None, None),
            P(None, "shard", None),
            P(None, "shard", None),
            P(None, "shard", None),
            P(None, "shard", None),
            P(None, None, "shard"),
            P(None, None, "shard"),
            P(None, None, "shard"),
            P(None, "shard"),
            P(),
        ),
        check_vma=False,
    )
```

profile of v0, /device:TPU:0, one launch (start us, length us, event | category | flops | bytes accessed | tf_op | source)
XLA Modules:
  0.0 1341.8 jit_solution(16533433941194631323)
XLA Ops:
  17.5 24.0 %all-gather = bf16[1,2,512]{1,0,2:T(2,128)(2,1)S(1)} all-gather(bf16[1,2,32]{1,0,2:T(2,128)(2,1)S(1)} %copy.412), channel_id=2, replica_groups=mesh['rep'=2,'shard'=16] {'shard'}, dimensions={2}, use_global_device_ids=true | all-gather | bytes 2176 | tf_op jit(solution)/shard_map/all_gather | solution.py:134
  44.6 18.3 %all-gather.1 = bf16[1,2,512]{1,0,2:T(2,128)(2,1)S(1)} all-gather(bf16[1,2,32]{1,0,2:T(2,128)(2,1)S(1)} %copy.413), channel_id=3, replica_groups=mesh['rep'=2,'shard'=16] {'shard'}, dimensions={2}, use_global_device_ids=true | all-gather | bytes 2176 | tf_op jit(solution)/shard_map/all_gather | solution.py:135
  67.9 20.7 %all-gather.3 = bf16[1,4,512]{1,0,2:T(2,128)(2,1)S(1)} all-gather(bf16[1,4,32]{1,0,2:T(2,128)(2,1)S(1)} %copy.414), channel_id=5, replica_groups=mesh['rep'=2,'shard'=16] {'shard'}, dimensions={2}, use_global_device_ids=true | all-gather | bytes 4352 | tf_op jit(solution)/shard_map/all_gather | solution.py:136
  96.1 19.4 %all-gather.4 = bf16[1,512,512]{2,1,0:T(8,128)(2,1)S(1)} all-gather(bf16[1,32,512]{2,1,0:T(8,128)(2,1)S(1)} %get-tuple-element.155), channel_id=6, replica_groups=mesh['rep'=2,'shard'=16] {'shard'}, dimensions={1}, use_global_device_ids=true | all-gather | bytes 557056 | tf_op jit(solution)/shard_map/all_gather | solution.py:133
  115.5 18.6 %all-gather.6 = bf16[1,2048]{1,0:T(2,128)(2,1)S(1)} all-gather(bf16[1,128]{1,0:T(2,128)(2,1)S(1)} %get-tuple-element.163), channel_id=8, replica_groups=mesh['rep'=2,'shard'=16] {'shard'}, dimensions={1}, use_global_device_ids=true | all-gather | bytes 4352 | tf_op jit(solution)/shard_map/all_gather | solution.py:141
  134.3 18.2 %all-gather.8 = bf16[1,2,512]{1,0,2:T(2,128)(2,1)S(1)} all-gather(bf16[1,2,32]{1,0,2:T(2,128)(2,1)S(1)} %copy.415), channel_id=10, replica_groups=mesh['rep'=2,'shard'=16] {'shard'}, dimensions={2}, use_global_device_ids=true | all-gather | bytes 2176 | tf_op jit(solution)/shard_map/all_gather | solution.py:134
  156.2 19.6 %all-gather.9 = bf16[1,2,512]{1,0,2:T(2,128)(2,1)S(1)} all-gather(bf16[1,2,32]{1,0,2:T(2,128)(2,1)S(1)} %copy.416), channel_id=11, replica_groups=mesh['rep'=2,'shard'=16] {'shard'}, dimensions={2}, use_global_device_ids=true | all-gather | bytes 2176 | tf_op jit(solution)/shard_map/all_gather | solution.py:135
  179.4 31.4 %all-gather.11 = bf16[1,4,512]{1,0,2:T(2,128)(2,1)S(1)} all-gather(bf16[1,4,32]{1,0,2:T(2,128)(2,1)S(1)} %copy.417), channel_id=13, replica_groups=mesh['rep'=2,'shard'=16] {'shard'}, dimensions={2}, use_global_device_ids=true | all-gather | bytes 4352 | tf_op jit(solution)/shard_map/all_gather | solution.py:136
  220.6 21.8 %all-gather.12 = bf16[1,512,512]{2,1,0:T(8,128)(2,1)} all-gather(bf16[1,32,512]{2,1,0:T(8,128)(2,1)S(1)} %get-tuple-element.154), channel_id=14, replica_groups=mesh['rep'=2,'shard'=16] {'shard'}, dimensions={1}, use_global_device_ids=true | all-gather | bytes 557056 | tf_op jit(solution)/shard_map/all_gather | solution.py:133
  497.7 31.7 %all-reduce.2 = (bf16[2048]{0:T(1024)(128)(2,1)S(1)}, bf16[2048]{0:T(1024)(128)(2,1)S(1)}) all-reduce(bf16[2048]{0:T(1024)(128)(2,1)S(1)} %copy-done.107, bf16[2048]{0:T(1024)(128)(2,1)S(1)} %copy-done.108), channel_id=33, replica_groups=mesh['rep'=2,'shard'=16] {'shard'}, use_global_device_ids=true, to_apply=%region_63.64.clone | all-reduce | flops 4096 | bytes 16384
  534.4 37.7 %psum.71 = f32[2,169,16]{1,2,0:T(8,128)} all-reduce(f32[2,169,16]{1,2,0:T(8,128)S(1)} %pad_maximum_fusion.10), channel_id=1, replica_groups=mesh['rep'=2,'shard'=16] {'rep','shard'}, use_global_device_ids=true, to_apply=%region_67.68 | all-reduce | flops 5408 | bytes 43264 | tf_op jit(solution)/shard_map/psum | solution.py:340
  573.6 53.1 %reduce-scatter.27.cloned.1.call-done = bf16[32,1536]{1,0:T(8,128)(2,1)} async-done(((bf16[512,1536]{1,0:T(8,128)(2,1)}), bf16[32,1536]{1,0:T(8,128)(2,1)}) %reduce-scatter.27.cloned.1.call-update) | async-done | bytes 98320 | tf_op jit(solution)/shard_map/reduce_scatter | solution.py:301
  626.7 62.5 %reduce-scatter.29.cloned.1.call-done = bf16[32,1536]{1,0:T(8,128)(2,1)} async-done(((bf16[512,1536]{1,0:T(8,128)(2,1)}), bf16[32,1536]{1,0:T(8,128)(2,1)}) %reduce-scatter.29.cloned.1.call-update) | async-done | bytes 98320 | tf_op jit(solution)/shard_map/reduce_scatter | solution.py:301
  690.8 62.7 %reduce-scatter.37.cloned.1.call-done = bf16[32,2048]{1,0:T(8,128)(2,1)} async-done(((bf16[512,2048]{1,0:T(8,128)(2,1)}), bf16[32,2048]{1,0:T(8,128)(2,1)}) %reduce-scatter.37.cloned.1.call-update) | async-done | bytes 131088 | tf_op jit(solution)/shard_map/reduce_scatter | solution.py:318
  753.6 64.6 %reduce-scatter.35.cloned.1.call-done = bf16[32,2048]{1,0:T(8,128)(2,1)} async-done(((bf16[512,2048]{1,0:T(8,128)(2,1)}), bf16[32,2048]{1,0:T(8,128)(2,1)}) %reduce-scatter.35.cloned.1.call-update) | async-done | bytes 131088 | tf_op jit(solution)/shard_map/reduce_scatter | solution.py:318
  819.9 62.6 %reduce-scatter.39.cloned.1.call-done = bf16[128,512]{1,0:T(8,128)(2,1)} async-done(((bf16[2048,512]{1,0:T(8,128)(2,1)}), bf16[128,512]{1,0:T(8,128)(2,1)}) %reduce-scatter.39.cloned.1.call-update) | async-done | bytes 131088 | tf_op jit(solution)/shard_map/reduce_scatter | solution.py:321
  882.4 64.7 %reduce-scatter.41.cloned.1.call-done = bf16[128,512]{1,0:T(8,128)(2,1)} async-done(((bf16[2048,512]{1,0:T(8,128)(2,1)}), bf16[128,512]{1,0:T(8,128)(2,1)}) %reduce-scatter.41.cloned.1.call-update) | async-done | bytes 131088 | tf_op jit(solution)/shard_map/reduce_scatter | solution.py:321
  950.1 54.4 %reduce-scatter.47.cloned.1.call-done = bf16[32,2]{1,0:T(8,128)(2,1)} async-done(((bf16[512,2]{1,0:T(8,128)(2,1)}), bf16[32,2]{1,0:T(8,128)(2,1)}) %reduce-scatter.47.cloned.1.call-update) | async-done | bytes 144
  1005.3 56.7 %reduce-scatter.49.cloned.1.call-done = bf16[32,2]{1,0:T(8,128)(2,1)} async-done(((bf16[512,2]{1,0:T(8,128)(2,1)}), bf16[32,2]{1,0:T(8,128)(2,1)}) %reduce-scatter.49.cloned.1.call-update) | async-done | bytes 144
  1062.8 56.7 %reduce-scatter.43.cloned.1.call-done = bf16[32,2]{1,0:T(8,128)(2,1)} async-done(((bf16[512,2]{1,0:T(8,128)(2,1)}), bf16[32,2]{1,0:T(8,128)(2,1)}) %reduce-scatter.43.cloned.1.call-update) | async-done | bytes 144
  1120.2 57.2 %reduce-scatter.45.cloned.1.call-done = bf16[32,2]{1,0:T(8,128)(2,1)} async-done(((bf16[512,2]{1,0:T(8,128)(2,1)}), bf16[32,2]{1,0:T(8,128)(2,1)}) %reduce-scatter.45.cloned.1.call-update) | async-done | bytes 144
  1178.3 56.8 %reduce-scatter.51.cloned.1.call-done = bf16[32,4]{1,0:T(8,128)(2,1)} async-done(((bf16[512,4]{1,0:T(8,128)(2,1)}), bf16[32,4]{1,0:T(8,128)(2,1)}) %reduce-scatter.51.cloned.1.call-update) | async-done | bytes 272
  1235.8 56.7 %reduce-scatter.53.cloned.1.call-done = bf16[32,4]{1,0:T(8,128)(2,1)} async-done(((bf16[512,4]{1,0:T(8,128)(2,1)}), bf16[32,4]{1,0:T(8,128)(2,1)}) %reduce-scatter.53.cloned.1.call-update) | async-done | bytes 272
  1300.6 28.8 %all-reduce.7.cloned.1.call-done = (bf16[2,32,1536]{2,1,0:T(8,128)(2,1)}, bf16[2,32,512]{2,1,0:T(8,128)(2,1)}, bf16[2,32,2048]{2,1,0:T(8,128)(2,1)}, bf16[2,128,512]{2,1,0:T(8,128)(2,1)}) async-done(((bf16[2,32,1536]{2,1,0:T(8,128)(2,1)}, bf16[2,32,512]{2,1,0:T(8,128)(2,1)}, bf16[2,32,2048]{2,1,0:T(8,128)(2,1)}, bf16[2,128,512]{2,1,0:T(8,128)(2,1)}), (bf16[2,32,1536]{2,1,0:T(8,128)(2,1)}, ...) | async-done | bytes 786448 | tf_op jit(solution)/shard_map/psum | solution.py:71
  (556 shorter events, 325.5 us)
Async XLA Ops:
  7.2 253.9 %all-gather.23.cloned.1.call-start = ((), (), s32[]{:S(2)}) async-start(), calls=%async_computation.22 | async-start | bytes 1671168 | tf_op jit(solution)/shard_map/all_gather | solution.py:132
  8.9 275.0 %all-gather.25.cloned.1.call-start = ((), (), s32[]{:S(2)}) async-start(), calls=%async_computation.23 | async-start | bytes 2228224 | tf_op jit(solution)/shard_map/all_gather | solution.py:139
  10.7 280.6 %all-gather.27.cloned.1.call-start = ((), (), s32[]{:S(2)}) async-start(), calls=%async_computation.24 | async-start | bytes 2228224 | tf_op jit(solution)/shard_map/all_gather | solution.py:140
  12.4 288.5 %all-gather.29.cloned.1.call-start = ((), (), s32[]{:S(2)}) async-start(), calls=%async_computation.25 | async-start | bytes 1671168 | tf_op jit(solution)/shard_map/all_gather | solution.py:132
  13.0 321.2 %all-gather.31.cloned.1.call-start = ((), (), s32[]{:S(2)}) async-start(), calls=%async_computation.26 | async-start | bytes 2228224 | tf_op jit(solution)/shard_map/all_gather | solution.py:139
  13.6 327.7 %all-gather.33.cloned.1.call-start = ((), (), s32[]{:S(2)}) async-start(), calls=%async_computation.27 | async-start | bytes 2228224 | tf_op jit(solution)/shard_map/all_gather | solution.py:140
  14.2 558.0 %reduce-scatter.33.cloned.1.call-start = ((), (), s32[]{:S(2)}) async-start(), calls=%async_computation.17 | async-start | bytes 557056 | tf_op jit(solution)/shard_map/reduce_scatter | solution.py:304
  44.5 238.0 %copy-start.81 = (f32[512]{0:T(512)}, f32[512]{0:T(512)S(1)}, u32[]{:S(2)}) copy-start(f32[512]{0:T(512)S(1)} %get-tuple-element.101) | copy-start | bytes 6148
  67.8 193.3 %copy-start.39 = (bf16[196,512]{1,0:T(8,128)(2,1)}, bf16[196,512]{1,0:T(8,128)(2,1)S(1)}, u32[]{:S(2)}) copy-start(bf16[196,512]{1,0:T(8,128)(2,1)S(1)} %reshape_reshape.24) | copy-start | bytes 602116
  450.9 121.3 %reduce-scatter.31.cloned.1.call-start = ((), (), s32[]{:S(2)}) async-start(), calls=%async_computation.16 | async-start | bytes 557056 | tf_op jit(solution)/shard_map/reduce_scatter | solution.py:304
  460.2 166.5 %reduce-scatter.27.cloned.1.call-start = ((), (), s32[]{:S(2)}) async-start(), calls=%async_computation.14 | async-start | bytes 1671168 | tf_op jit(solution)/shard_map/reduce_scatter | solution.py:301
  466.2 223.0 %reduce-scatter.29.cloned.1.call-start = ((), (), s32[]{:S(2)}) async-start(), calls=%async_computation.15 | async-start | bytes 1671168 | tf_op jit(solution)/shard_map/reduce_scatter | solution.py:301
  468.1 285.4 %reduce-scatter.37.cloned.1.call-start = ((), (), s32[]{:S(2)}) async-start(), calls=%async_computation.19 | async-start | bytes 2228224 | tf_op jit(solution)/shard_map/reduce_scatter | solution.py:318
  471.4 346.8 %reduce-scatter.35.cloned.1.call-start = ((), (), s32[]{:S(2)}) async-start(), calls=%async_computation.18 | async-start | bytes 2228224 | tf_op jit(solution)/shard_map/reduce_scatter | solution.py:318
  474.6 407.8 %reduce-scatter.39.cloned.1.call-start = ((), (), s32[]{:S(2)}) async-start(), calls=%async_computation.20 | async-start | bytes 2228224 | tf_op jit(solution)/shard_map/reduce_scatter | solution.py:321
  478.0 469.1 %reduce-scatter.41.cloned.1.call-start = ((), (), s32[]{:S(2)}) async-start(), calls=%async_computation.21 | async-start | bytes 2228224 | tf_op jit(solution)/shard_map/reduce_scatter | solution.py:321
  481.4 523.2 %reduce-scatter.47.cloned.1.call-start = ((), (), s32[]{:S(2)}) async-start(), calls=%async_computation.30 | async-start | bytes 139264
  496.8 565.2 %reduce-scatter.49.cloned.1.call-start = ((), (), s32[]{:S(2)}) async-start(), calls=%async_computation.31 | async-start | bytes 139264
  529.4 590.0 %reduce-scatter.43.cloned.1.call-start = ((), (), s32[]{:S(2)}) async-start(), calls=%async_computation.28 | async-start | bytes 139264
  530.4 647.1 %reduce-scatter.45.cloned.1.call-start = ((), (), s32[]{:S(2)}) async-start(), calls=%async_computation.29 | async-start | bytes 139264
  531.8 703.2 %reduce-scatter.51.cloned.1.call-start = ((), (), s32[]{:S(2)}) async-start(), calls=%async_computation.32 | async-start | bytes 139264
  533.6 415.3 %copy-start.34 = (f32[1,14,14,512]{3,0,2,1:T(1,128)S(1)}, f32[1,14,14,512]{3,0,2,1:T(1,128)}, u32[]{:S(2)}) copy-start(f32[1,14,14,512]{3,0,2,1:T(1,128)} %get-tuple-element.127) | copy-start | bytes 1204228
  534.3 758.2 %reduce-scatter.53.cloned.1.call-start = ((), (), s32[]{:S(2)}) async-start(), calls=%async_computation.33 | async-start | bytes 139264
  572.1 757.3 %all-reduce.7.cloned.1.call-start = ((), (), s32[]{:S(2)}) async-start(), calls=%async_computation.34 | async-start | bytes 1572864 | tf_op jit(solution)/shard_map/psum | solution.py:71
  (113 other events, 1343.8 us)
Sparse Core Ops, SparseCore 0:
  10.9 42.7 all-gather.22
  56.4 40.3 all-gather.24
  99.5 40.4 all-gather.26
  142.1 38.9 all-gather.28
  183.7 40.5 all-gather.30
  226.9 40.4 all-gather.32
  451.1 53.9 reduce-scatter.32
  509.6 54.7 reduce-scatter.30
  568.1 58.5 reduce-scatter.26
  630.6 58.4 reduce-scatter.28
  692.9 60.5 reduce-scatter.36
  757.6 60.5 reduce-scatter.34
  821.9 60.4 reduce-scatter.38
  886.5 60.5 reduce-scatter.40
  950.4 54.0 reduce-scatter.46
  1007.8 54.1 reduce-scatter.48
  1065.3 54.0 reduce-scatter.42
  1123.3 54.0 reduce-scatter.44
  1180.9 54.0 reduce-scatter.50
  1238.3 54.0 reduce-scatter.52
  1295.5 33.8 all-reduce.6
where the time goes:
time: 1350 us; the launch traced here: 1340 us
  waiting for transfers between devices  739 us (55%)
  blocking collectives  284 us (21%)
  local copies, waits for them, and re-layouts  132 us (10%)
  other arithmetic  84.2 us (6%)
  matrix products  84.1 us (6%)
  between operations  17.4 us (1%)
    unnamed x27, waiting for transfers between devices  340 us
    reduce_scatter x2, waiting for transfers between devices, body(): lax.psum_scatter(grad_w_first.astype(jnp.bfloat16), 'shard', scatter_dime...  127 us
    reduce_scatter x2, waiting for transfers between devices, body(): lax.psum_scatter(grad_w_second.astype(jnp.bfloat16), 'shard', scatter_dim...  127 us
    reduce_scatter x2, waiting for transfers between devices, body(): lax.psum_scatter(grad_w_proj_qkv.astype(jnp.bfloat16), 'shard', scatter_d...  116 us
    all_gather x2, blocking collectives, body(): lax.all_gather(branch_biases[layer_num], 'shard', axis=1, tiled=True)  52.1 us
    all_gather x2, blocking collectives, body(): lax.all_gather(norm_gains[layer_num], 'shard', axis=1, tiled=True)  42.1 us
    all_gather x2, blocking collectives, body(): lax.all_gather(w_proj[layer_num], 'shard', axis=0, tiled=True)  41.2 us
    all_gather x2, blocking collectives, body(): lax.all_gather(norm_shifts[layer_num], 'shard', axis=1, tiled=True)  37.8 us
  transfers between devices with their start and end apart: 21, of which 13 were waited for; matrix products, arithmetic and copies ran while one was open for 13% of the time, Pallas kernels for 0%

commit v1 on v0

--- a/solution.py
+++ b/solution.py
@@ -10,6 +10,24 @@
 highest = lax.Precision.HIGHEST
 inv_root_two = 0.7071067811865476
 inv_root_two_pi = 0.3989422804014327
+
+
+def ring_gather(array, axis, dim):
+    ways, here, step = (lax.axis_size(axis), lax.axis_index(axis), array.shape[dim])
+    shape = [n * ways if d == dim else n for d, n in enumerate(array.shape)]
+    full = lax.dynamic_update_slice_in_dim(
+        jnp.zeros(shape, array.dtype), array, here * step, axis=dim
+    )
+    going_up = going_down = array
+    for far in range(1, ways // 2 + 1):
+        going_up = lax.ppermute(going_up, axis, [(d, (d + 1) % ways) for d in range(ways)])
+        full = lax.dynamic_update_slice_in_dim(full, going_up, (here - far) % ways * step, axis=dim)
+        if 2 * far < ways:
+            going_down = lax.ppermute(going_down, axis, [(d, (d - 1) % ways) for d in range(ways)])
+            full = lax.dynamic_update_slice_in_dim(
+                full, going_down, (here + far) % ways * step, axis=dim
+            )
+    return full
 
 
 def layer_norm(values, norm_gain, norm_shift):
@@ -138,7 +156,7 @@
         mlp_w = (
             lax.all_gather(w_fc1[layer_num], "shard", axis=0, tiled=True),
             lax.all_gather(w_fc2[layer_num], "shard", axis=0, tiled=True),
-            lax.all_gather(fc1_bias[layer_num], "shard", axis=0, tiled=True),
+            ring_gather(fc1_bias[layer_num], "shard", 0),
         )
         kept_weights.append((attn_w, mlp_w))
         wqkv, wproj, gains, shifts, biases = attn_w

time: 1350 us -> 1370 us (1.015)
  starting transfers between devices: 1.33 us -> 64.7 us
  blocking collectives: 284 us -> 231 us
    ppermute x0 -> x30, starting transfers between devices: none -> 63.3 us  [the longest x14 62.2 us: ring_gather(): lax.ppermute(going_down, axis, [(d, (d - 1) % ways) for d in range(ways)])]
    all_gather x2 -> x0, blocking collectives: 36 us -> none  [body(): lax.all_gather(fc1_bias[layer_num], 'shard', axis=0, tiled=True)]
    all_gather x2, blocking collectives: 52.1 us -> 37.8 us  [body(): lax.all_gather(branch_biases[layer_num], 'shard', axis=1, tiled=True)]
  transfers between devices with their start and end apart: 21 -> 51, of which waited for: 13 -> 16; matrix products, arithmetic and copies ran while one was open for 13% -> 13% of each run, Pallas kernels for 0% -> 0%
where the time goes in v1:
time: 1370 us; the launch traced here: 1360 us
  waiting for transfers between devices  744 us (54%)
  blocking collectives  231 us (17%)
  local copies, waits for them, and re-layouts  138 us (10%)
  matrix products  84.6 us (6%)
  other arithmetic  84 us (6%)
  starting transfers between devices  64.7 us (5%)
  between operations  17.6 us (1%)
    unnamed x27, waiting for transfers between devices  340 us
    reduce_scatter x2, waiting for transfers between devices, body(): lax.psum_scatter(grad_w_first.astype(jnp.bfloat16), 'shard', scatter_dime...  127 us
    reduce_scatter x2, waiting for transfers between devices, body(): lax.psum_scatter(grad_w_second.astype(jnp.bfloat16), 'shard', scatter_dim...  127 us
    reduce_scatter x2, waiting for transfers between devices, body(): lax.psum_scatter(grad_w_proj_qkv.astype(jnp.bfloat16), 'shard', scatter_d...  116 us
    ppermute x14, starting transfers between devices, ring_gather(): lax.ppermute(going_down, axis, [(d, (d - 1) % ways) for d in range(ways)])  62.2 us
    all_gather x2, blocking collectives, body(): lax.all_gather(w_proj[layer_num], 'shard', axis=0, tiled=True)  43.8 us
    all_gather x2, blocking collectives, body(): lax.all_gather(norm_shifts[layer_num], 'shard', axis=1, tiled=True)  40.1 us
    all_gather x2, blocking collectives, body(): lax.all_gather(branch_biases[layer_num], 'shard', axis=1, tiled=True)  37.8 us
  transfers between devices with their start and end apart: 51, of which 16 were waited for; matrix products, arithmetic and copies ran while one was open for 13% of the time, Pallas kernels for 0%

profile of v1, /device:TPU:0, one launch (start us, length us, event | category | flops | bytes accessed | tf_op | source)
XLA Modules:
  0.0 1364.6 jit_solution(8623569379943190570)
XLA Ops:
  27.3 18.0 %all-gather = bf16[1,2,512]{1,0,2:T(2,128)(2,1)S(1)} all-gather(bf16[1,2,32]{1,0,2:T(2,128)(2,1)S(1)} %copy.412), channel_id=2, replica_groups=mesh['rep'=2,'shard'=16] {'shard'}, dimensions={2}, use_global_device_ids=true | all-gather | bytes 2176 | tf_op jit(solution)/shard_map/all_gather | solution.py:152
  48.5 20.2 %all-gather.1 = bf16[1,2,512]{1,0,2:T(2,128)(2,1)S(1)} all-gather(bf16[1,2,32]{1,0,2:T(2,128)(2,1)S(1)} %copy.413), channel_id=3, replica_groups=mesh['rep'=2,'shard'=16] {'shard'}, dimensions={2}, use_global_device_ids=true | all-gather | bytes 2176 | tf_op jit(solution)/shard_map/all_gather | solution.py:153
  73.7 18.9 %all-gather.3 = bf16[1,4,512]{1,0,2:T(2,128)(2,1)S(1)} all-gather(bf16[1,4,32]{1,0,2:T(2,128)(2,1)S(1)} %copy.414), channel_id=5, replica_groups=mesh['rep'=2,'shard'=16] {'shard'}, dimensions={2}, use_global_device_ids=true | all-gather | bytes 4352 | tf_op jit(solution)/shard_map/all_gather | solution.py:154
  100.2 21.6 %all-gather.4 = bf16[1,512,512]{2,1,0:T(8,128)(2,1)S(1)} all-gather(bf16[1,32,512]{2,1,0:T(8,128)(2,1)S(1)} %get-tuple-element.155), channel_id=6, replica_groups=mesh['rep'=2,'shard'=16] {'shard'}, dimensions={1}, use_global_device_ids=true | all-gather | bytes 557056 | tf_op jit(solution)/shard_map/all_gather | solution.py:151
  121.8 18.5 %all-gather.7 = bf16[1,2,512]{1,0,2:T(2,128)(2,1)S(1)} all-gather(bf16[1,2,32]{1,0,2:T(2,128)(2,1)S(1)} %copy.415), channel_id=9, replica_groups=mesh['rep'=2,'shard'=16] {'shard'}, dimensions={2}, use_global_device_ids=true | all-gather | bytes 2176 | tf_op jit(solution)/shard_map/all_gather | solution.py:152
  144.0 19.9 %all-gather.8 = bf16[1,2,512]{1,0,2:T(2,128)(2,1)S(1)} all-gather(bf16[1,2,32]{1,0,2:T(2,128)(2,1)S(1)} %copy.416), channel_id=10, replica_groups=mesh['rep'=2,'shard'=16] {'shard'}, dimensions={2}, use_global_device_ids=true | all-gather | bytes 2176 | tf_op jit(solution)/shard_map/all_gather | solution.py:153
  167.6 18.9 %all-gather.10 = bf16[1,4,512]{1,0,2:T(2,128)(2,1)S(1)} all-gather(bf16[1,4,32]{1,0,2:T(2,128)(2,1)S(1)} %copy.417), channel_id=12, replica_groups=mesh['rep'=2,'shard'=16] {'shard'}, dimensions={2}, use_global_device_ids=true | all-gather | bytes 4352 | tf_op jit(solution)/shard_map/all_gather | solution.py:154
  186.8 7.3 slice_reduce_fusion
  196.2 22.3 %all-gather.11 = bf16[1,512,512]{2,1,0:T(8,128)(2,1)} all-gather(bf16[1,32,512]{2,1,0:T(8,128)(2,1)S(1)} %get-tuple-element.154), channel_id=13, replica_groups=mesh['rep'=2,'shard'=16] {'shard'}, dimensions={1}, use_global_device_ids=true | all-gather | bytes 557056 | tf_op jit(solution)/shard_map/all_gather | solution.py:151
  522.0 30.0 %all-reduce.2 = (bf16[2048]{0:T(1024)(128)(2,1)S(1)}, bf16[2048]{0:T(1024)(128)(2,1)S(1)}) all-reduce(bf16[2048]{0:T(1024)(128)(2,1)S(1)} %copy-done.107, bf16[2048]{0:T(1024)(128)(2,1)S(1)} %copy-done.108), channel_id=31, replica_groups=mesh['rep'=2,'shard'=16] {'shard'}, use_global_device_ids=true, to_apply=%region_63.64.clone | all-reduce | flops 4096 | bytes 16384
  557.1 37.7 %psum.71 = f32[2,169,16]{1,2,0:T(8,128)} all-reduce(f32[2,169,16]{1,2,0:T(8,128)S(1)} %pad_maximum_fusion.10), channel_id=1, replica_groups=mesh['rep'=2,'shard'=16] {'rep','shard'}, use_global_device_ids=true, to_apply=%region_67.68 | all-reduce | flops 5408 | bytes 43264 | tf_op jit(solution)/shard_map/psum | solution.py:358
  596.3 53.3 %reduce-scatter.27.cloned.1.call-done = bf16[32,1536]{1,0:T(8,128)(2,1)} async-done(((bf16[512,1536]{1,0:T(8,128)(2,1)}), bf16[32,1536]{1,0:T(8,128)(2,1)}) %reduce-scatter.27.cloned.1.call-update) | async-done | bytes 98320 | tf_op jit(solution)/shard_map/reduce_scatter | solution.py:319
  649.5 62.5 %reduce-scatter.29.cloned.1.call-done = bf16[32,1536]{1,0:T(8,128)(2,1)} async-done(((bf16[512,1536]{1,0:T(8,128)(2,1)}), bf16[32,1536]{1,0:T(8,128)(2,1)}) %reduce-scatter.29.cloned.1.call-update) | async-done | bytes 98320 | tf_op jit(solution)/shard_map/reduce_scatter | solution.py:319
  713.7 62.8 %reduce-scatter.37.cloned.1.call-done = bf16[32,2048]{1,0:T(8,128)(2,1)} async-done(((bf16[512,2048]{1,0:T(8,128)(2,1)}), bf16[32,2048]{1,0:T(8,128)(2,1)}) %reduce-scatter.37.cloned.1.call-update) | async-done | bytes 131088 | tf_op jit(solution)/shard_map/reduce_scatter | solution.py:336
  776.4 64.7 %reduce-scatter.35.cloned.1.call-done = bf16[32,2048]{1,0:T(8,128)(2,1)} async-done(((bf16[512,2048]{1,0:T(8,128)(2,1)}), bf16[32,2048]{1,0:T(8,128)(2,1)}) %reduce-scatter.35.cloned.1.call-update) | async-done | bytes 131088 | tf_op jit(solution)/shard_map/reduce_scatter | solution.py:336
  842.8 62.7 %reduce-scatter.39.cloned.1.call-done = bf16[128,512]{1,0:T(8,128)(2,1)} async-done(((bf16[2048,512]{1,0:T(8,128)(2,1)}), bf16[128,512]{1,0:T(8,128)(2,1)}) %reduce-scatter.39.cloned.1.call-update) | async-done | bytes 131088 | tf_op jit(solution)/shard_map/reduce_scatter | solution.py:339
  905.4 64.7 %reduce-scatter.41.cloned.1.call-done = bf16[128,512]{1,0:T(8,128)(2,1)} async-done(((bf16[2048,512]{1,0:T(8,128)(2,1)}), bf16[128,512]{1,0:T(8,128)(2,1)}) %reduce-scatter.41.cloned.1.call-update) | async-done | bytes 131088 | tf_op jit(solution)/shard_map/reduce_scatter | solution.py:339
  973.1 54.5 %reduce-scatter.47.cloned.1.call-done = bf16[32,2]{1,0:T(8,128)(2,1)} async-done(((bf16[512,2]{1,0:T(8,128)(2,1)}), bf16[32,2]{1,0:T(8,128)(2,1)}) %reduce-scatter.47.cloned.1.call-update) | async-done | bytes 144
  1028.4 56.7 %reduce-scatter.49.cloned.1.call-done = bf16[32,2]{1,0:T(8,128)(2,1)} async-done(((bf16[512,2]{1,0:T(8,128)(2,1)}), bf16[32,2]{1,0:T(8,128)(2,1)}) %reduce-scatter.49.cloned.1.call-update) | async-done | bytes 144
  1085.8 56.6 %reduce-scatter.43.cloned.1.call-done = bf16[32,2]{1,0:T(8,128)(2,1)} async-done(((bf16[512,2]{1,0:T(8,128)(2,1)}), bf16[32,2]{1,0:T(8,128)(2,1)}) %reduce-scatter.43.cloned.1.call-update) | async-done | bytes 144
  1143.2 57.3 %reduce-scatter.45.cloned.1.call-done = bf16[32,2]{1,0:T(8,128)(2,1)} async-done(((bf16[512,2]{1,0:T(8,128)(2,1)}), bf16[32,2]{1,0:T(8,128)(2,1)}) %reduce-scatter.45.cloned.1.call-update) | async-done | bytes 144
  1201.3 56.8 %reduce-scatter.51.cloned.1.call-done = bf16[32,4]{1,0:T(8,128)(2,1)} async-done(((bf16[512,4]{1,0:T(8,128)(2,1)}), bf16[32,4]{1,0:T(8,128)(2,1)}) %reduce-scatter.51.cloned.1.call-update) | async-done | bytes 272
  1258.9 56.6 %reduce-scatter.53.cloned.1.call-done = bf16[32,4]{1,0:T(8,128)(2,1)} async-done(((bf16[512,4]{1,0:T(8,128)(2,1)}), bf16[32,4]{1,0:T(8,128)(2,1)}) %reduce-scatter.53.cloned.1.call-update) | async-done | bytes 272
  1323.6 28.9 %all-reduce.7.cloned.1.call-done = (bf16[2,32,1536]{2,1,0:T(8,128)(2,1)}, bf16[2,32,512]{2,1,0:T(8,128)(2,1)}, bf16[2,32,2048]{2,1,0:T(8,128)(2,1)}, bf16[2,128,512]{2,1,0:T(8,128)(2,1)}) async-done(((bf16[2,32,1536]{2,1,0:T(8,128)(2,1)}, bf16[2,32,512]{2,1,0:T(8,128)(2,1)}, bf16[2,32,2048]{2,1,0:T(8,128)(2,1)}, bf16[2,128,512]{2,1,0:T(8,128)(2,1)}), (bf16[2,32,1536]{2,1,0:T(8,128)(2,1)}, ...) | async-done | bytes 786448 | tf_op jit(solution)/shard_map/psum | solution.py:89
  (648 shorter events, 375.9 us)
Async XLA Ops:
  7.2 277.9 %all-gather.21.cloned.1.call-start = ((), (), s32[]{:S(2)}) async-start(), calls=%async_computation.22 | async-start | bytes 1671168 | tf_op jit(solution)/shard_map/all_gather | solution.py:150
  8.9 299.0 %all-gather.23.cloned.1.call-start = ((), (), s32[]{:S(2)}) async-start(), calls=%async_computation.23 | async-start | bytes 2228224 | tf_op jit(solution)/shard_map/all_gather | solution.py:157
  10.7 304.3 %all-gather.25.cloned.1.call-start = ((), (), s32[]{:S(2)}) async-start(), calls=%async_computation.24 | async-start | bytes 2228224 | tf_op jit(solution)/shard_map/all_gather | solution.py:158
  12.5 312.1 %all-gather.27.cloned.1.call-start = ((), (), s32[]{:S(2)}) async-start(), calls=%async_computation.25 | async-start | bytes 1671168 | tf_op jit(solution)/shard_map/all_gather | solution.py:150
  13.0 345.1 %all-gather.29.cloned.1.call-start = ((), (), s32[]{:S(2)}) async-start(), calls=%async_computation.26 | async-start | bytes 2228224 | tf_op jit(solution)/shard_map/all_gather | solution.py:157
  13.6 351.5 %all-gather.31.cloned.1.call-start = ((), (), s32[]{:S(2)}) async-start(), calls=%async_computation.27 | async-start | bytes 2228224 | tf_op jit(solution)/shard_map/all_gather | solution.py:158
  13.7 205.9 %collective-permute-start = (bf16[128]{0:T(256)(128)(2,1)S(1)}, bf16[128]{0:T(256)(128)(2,1)S(1)}, u32[]{:S(2)}, u32[]{:S(2)}) collective-permute-start(bf16[128]{0:T(256)(128)(2,1)S(1)} %get-tuple-element.163), channel_id=1, source_target_pairs={{0,1},{1,2},{2,3},{3,4},{4,5},{5,6},{6,7},{7,8},{8,9},{9,10},{10,1... | collective-permute-start | bytes 776 | tf_op jit(solution)/shard_map/ppermute | solution.py:23
  14.2 205.8 %collective-permute-start.1 = (bf16[128]{0:T(256)(128)(2,1)S(1)}, bf16[128]{0:T(256)(128)(2,1)S(1)}, u32[]{:S(2)}, u32[]{:S(2)}) collective-permute-start(bf16[128]{0:T(256)(128)(2,1)S(1)} %get-tuple-element.163), channel_id=1, source_target_pairs={{0,15},{1,0},{2,1},{3,2},{4,3},{5,4},{6,5},{7,6},{8,7},{9,8},{10,9... | collective-permute-start | bytes 776 | tf_op jit(solution)/shard_map/ppermute | solution.py:26
  19.2 204.8 %collective-permute-start.15 = (bf16[128]{0:T(256)(128)(2,1)S(1)}, bf16[128]{0:T(256)(128)(2,1)S(1)}, u32[]{:S(2)}, u32[]{:S(2)}) collective-permute-start(bf16[128]{0:T(256)(128)(2,1)S(1)} %get-tuple-element.162), channel_id=1, source_target_pairs={{0,1},{1,2},{2,3},{3,4},{4,5},{5,6},{6,7},{7,8},{8,9},{9,10},{10,1... | collective-permute-start | bytes 776 | tf_op jit(solution)/shard_map/ppermute | solution.py:23
  19.2 205.2 %collective-permute-start.16 = (bf16[128]{0:T(256)(128)(2,1)S(1)}, bf16[128]{0:T(256)(128)(2,1)S(1)}, u32[]{:S(2)}, u32[]{:S(2)}) collective-permute-start(bf16[128]{0:T(256)(128)(2,1)S(1)} %get-tuple-element.162), channel_id=1, source_target_pairs={{0,15},{1,0},{2,1},{3,2},{4,3},{5,4},{6,5},{7,6},{8,7},{9,8},{10,9... | collective-permute-start | bytes 776 | tf_op jit(solution)/shard_map/ppermute | solution.py:26
  23.7 571.1 %reduce-scatter.33.cloned.1.call-start = ((), (), s32[]{:S(2)}) async-start(), calls=%async_computation.17 | async-start | bytes 557056 | tf_op jit(solution)/shard_map/reduce_scatter | solution.py:322
  484.1 165.4 %reduce-scatter.27.cloned.1.call-start = ((), (), s32[]{:S(2)}) async-start(), calls=%async_computation.14 | async-start | bytes 1671168 | tf_op jit(solution)/shard_map/reduce_scatter | solution.py:319
  490.2 221.9 %reduce-scatter.29.cloned.1.call-start = ((), (), s32[]{:S(2)}) async-start(), calls=%async_computation.15 | async-start | bytes 1671168 | tf_op jit(solution)/shard_map/reduce_scatter | solution.py:319
  492.1 284.3 %reduce-scatter.37.cloned.1.call-start = ((), (), s32[]{:S(2)}) async-start(), calls=%async_computation.19 | async-start | bytes 2228224 | tf_op jit(solution)/shard_map/reduce_scatter | solution.py:336
  495.3 345.7 %reduce-scatter.35.cloned.1.call-start = ((), (), s32[]{:S(2)}) async-start(), calls=%async_computation.18 | async-start | bytes 2228224 | tf_op jit(solution)/shard_map/reduce_scatter | solution.py:336
  498.6 406.8 %reduce-scatter.39.cloned.1.call-start = ((), (), s32[]{:S(2)}) async-start(), calls=%async_computation.20 | async-start | bytes 2228224 | tf_op jit(solution)/shard_map/reduce_scatter | solution.py:339
  501.9 468.2 %reduce-scatter.41.cloned.1.call-start = ((), (), s32[]{:S(2)}) async-start(), calls=%async_computation.21 | async-start | bytes 2228224 | tf_op jit(solution)/shard_map/reduce_scatter | solution.py:339
  505.3 522.3 %reduce-scatter.47.cloned.1.call-start = ((), (), s32[]{:S(2)}) async-start(), calls=%async_computation.30 | async-start | bytes 139264
  521.1 563.9 %reduce-scatter.49.cloned.1.call-start = ((), (), s32[]{:S(2)}) async-start(), calls=%async_computation.31 | async-start | bytes 139264
  552.1 590.4 %reduce-scatter.43.cloned.1.call-start = ((), (), s32[]{:S(2)}) async-start(), calls=%async_computation.28 | async-start | bytes 139264
  553.1 647.4 %reduce-scatter.45.cloned.1.call-start = ((), (), s32[]{:S(2)}) async-start(), calls=%async_computation.29 | async-start | bytes 139264
  554.5 703.6 %reduce-scatter.51.cloned.1.call-start = ((), (), s32[]{:S(2)}) async-start(), calls=%async_computation.32 | async-start | bytes 139264
  557.0 758.5 %reduce-scatter.53.cloned.1.call-start = ((), (), s32[]{:S(2)}) async-start(), calls=%async_computation.33 | async-start | bytes 139264
  594.8 757.7 %all-reduce.7.cloned.1.call-start = ((), (), s32[]{:S(2)}) async-start(), calls=%async_computation.34 | async-start | bytes 1572864 | tf_op jit(solution)/shard_map/psum | solution.py:89
  (143 other events, 2573.9 us)
Sparse Core Ops, SparseCore 0:
  10.9 42.5 all-gather.20
  56.3 41.4 all-gather.22
  100.5 41.1 all-gather.24
  143.8 40.6 all-gather.26
  187.1 40.6 all-gather.28
  230.4 40.1 all-gather.30
  474.8 53.0 reduce-scatter.32
  532.5 54.8 reduce-scatter.30
  591.0 58.4 reduce-scatter.26
  653.5 58.4 reduce-scatter.28
  715.8 60.6 reduce-scatter.36
  780.5 60.5 reduce-scatter.34
  844.8 60.5 reduce-scatter.38
  909.5 60.5 reduce-scatter.40
  973.4 54.1 reduce-scatter.46
  1030.9 54.0 reduce-scatter.48
  1088.3 54.0 reduce-scatter.42
  1146.3 54.1 reduce-scatter.44
  1203.9 54.0 reduce-scatter.50
  1261.4 54.0 reduce-scatter.52
  1318.5 33.8 all-reduce.6
